TPU v7x, 32 devices: a whole 2x2x4 slice. The times are simulated.
32 devices in a mesh: expert: 4 (over x, core), ctx: 2 (over y), tensor: 4 (over z).
Axes of the slice: x: 2, y: 2, z: 4, core: 2. Of those that a mesh axis runs over, the one named last changes fastest.
Arguments:
- tokens: bfloat16 [64, 6144], P('expert', 'tensor'), may hold values from -6 to 6
- expert_ids: int32 [64, 2], P('expert'), may hold values from 0 to 3, all different within a row; in each aligned block of 8 rows (0 to 7, 8 to 15, ...) at most 4 rows name the same one
- route_gates: float32 [64, 2], P('expert'), may hold values from 0.2 to 1
- up_weight: bfloat16 [4, 12288, 6144], P('expert', 'ctx', 'tensor'), may hold values from -0.078125 to 0.078125
- down_weight: bfloat16 [4, 12288, 6144], P('expert', 'ctx', 'tensor'), may hold values from -0.0546875 to 0.0546875
Outputs:
- mixed: bfloat16 [64, 6144], P(('expert', 'ctx'), 'tensor')
Inputs may be any that keep to these rules, and one draw needn't show every extreme that they name: `expert_ids`: each token names 2 different experts. In each aligned block of 8 tokens at most 4 choices name one expert, and in some block one expert is named exactly 4 times. Every expert is named somewhere.
All inputs are finite; a program needn't handle non-finite values.
Results may differ from a plain program's by a relative error of at most 0.0057.
Values may be sent and summed in bfloat16 or wider, within the bound.
No kernel may reach another device: no remote copies, remote signals or barrier semaphores. Data moves between devices by JAX's collectives and lax.ppermute only.
A program may use at most 64 MiB of HBM per device.

v0:
```python
import jax
import jax.numpy as jnp
from jax import lax
from jax.sharding import PartitionSpec as P


def choice_slots(expert_ids, block_len, expert_count):
    top_count = expert_ids.shape[1]
    per_block = expert_ids.reshape(-1, block_len * top_count)
    marked = (
        per_block[:, :, None] == jnp.arange(expert_count, dtype=jnp.int32)[None, None, :]
    ).astype(jnp.int32)
    earlier = jnp.cumsum(marked, axis=1) - marked
    return jnp.sum(earlier * marked, axis=2).reshape(-1, top_count)


def local(tokens, expert_ids, route_gates, up_weight, down_weight):
    ctx_count = lax.axis_size("ctx")
    expert_count = lax.axis_size("expert")
    group_len = tokens.shape[0]
    width_local = tokens.shape[1]
    block_len = group_len // ctx_count
    capacity = block_len // 2
    per_expert = ctx_count * capacity
    ctx_index = lax.axis_index("ctx")
    slot_ids = choice_slots(expert_ids, block_len, expert_count)
    block_of = (jnp.arange(group_len, dtype=jnp.int32) // block_len)[:, None]
    dest_index = expert_ids * per_expert + block_of * capacity + slot_ids
    slot_range = jnp.arange(expert_count * per_expert, dtype=jnp.int32)
    marked = jnp.sum(
        (dest_index[None, :, :] == slot_range[:, None, None]).astype(jnp.int32), axis=2
    )
    outgoing = jnp.dot(marked.astype(jnp.bfloat16), tokens, preferred_element_type=jnp.float32)
    outgoing = outgoing.astype(jnp.bfloat16).reshape(expert_count, per_expert, width_local)
    arrived = lax.all_to_all(outgoing, "expert", split_axis=0, concat_axis=0, tiled=True)
    row_data = arrived.reshape(-1, width_local)
    up_local = up_weight[0]
    down_local = down_weight[0]
    before_act = lax.dot_general(
        row_data, up_local, (((1,), (1,)), ((), ())), preferred_element_type=jnp.float32
    )
    share = lax.psum_scatter(before_act, "tensor", scatter_dimension=0, tiled=True)
    hidden = jnp.square(jnp.maximum(share, 0.0)).astype(jnp.bfloat16)
    projected = jnp.dot(
        lax.all_gather(hidden, "tensor", axis=0, tiled=True),
        down_local,
        preferred_element_type=jnp.float32,
    )
    by_block = projected.reshape(expert_count, ctx_count, capacity, width_local)
    totals = lax.psum(by_block, "ctx")
    own_rows = lax.dynamic_index_in_dim(totals, ctx_index, 1, keepdims=False)
    returned = lax.all_to_all(
        own_rows.astype(jnp.bfloat16), "expert", split_axis=0, concat_axis=0, tiled=True
    )
    flattened = returned.reshape(-1, width_local)
    first_row = ctx_index * block_len
    own_ids = lax.dynamic_slice_in_dim(expert_ids, first_row, block_len, 0)
    own_slots = lax.dynamic_slice_in_dim(slot_ids, first_row, block_len, 0)
    own_gates = lax.dynamic_slice_in_dim(route_gates, first_row, block_len, 0)
    row_index = own_ids * capacity + own_slots
    picked = jnp.take(flattened, row_index, axis=0).astype(jnp.float32)
    mixed = jnp.sum(own_gates[:, :, None] * picked, axis=1)
    return mixed.astype(jnp.bfloat16)


def solution(mesh):
    in_specs = (
        P("expert", "tensor"),
        P("expert", None),
        P("expert", None),
        P("expert", "ctx", "tensor"),
        P("expert", "ctx", "tensor"),
    )
    out_specs = P(("expert", "ctx"), "tensor")
    return jax.shard_map(local, mesh=mesh, in_specs=in_specs, out_specs=out_specs, check_vma=False)
```

profile of v0, /device:TPU:0, one launch (start us, length us, event | category | flops | bytes accessed | tf_op | source)
XLA Modules:
  0.0 106.3 jit_solution(8248955880566829928)
XLA Ops:
  6.5 0.0 copy-start
  6.5 0.0 reduce-scatter.2.cloned.1.call-start
  6.5 0.8 copy.26
  7.3 0.1 eq.28
  7.4 0.1 fusion.7
  7.5 0.2 select_reduce_fusion
  7.7 0.1 reshape.38
  7.8 0.1 copy.28
  7.9 0.7 add_add_fusion
  8.6 0.1 convert_reduce_fusion
  8.6 0.0 copy-done
  8.6 0.2 fusion.4
  8.8 8.3 %all_to_all.10 = bf16[4,8,1536]{2,1,0:T(8,128)(2,1)S(1)} all-to-all(bf16[4,8,1536]{2,1,0:T(8,128)(2,1)S(1)} %fusion.4), channel_id=1, replica_groups=mesh['expert'=4,'ctx'=2,'tensor'=4] {'expert'}, dimensions={0} | all-to-all | bytes 196608 | tf_op jit(solution)/shard_map/all_to_all | solution.py:35
  17.2 0.0 copy-start.1
  17.2 12.8 %fusion.2 = f32[32,6144]{1,0:T(8,128)} fusion(bf16[1,6144,1536]{2,1,0:T(8,128)(2,1)} %param.8, bf16[4,8,1536]{2,1,0:T(8,128)(2,1)S(1)} %all_to_all.10), kind=kOutput, calls=%fused_computation.3 | convolution fusion | flops 603979776 | bytes 19759104 | tf_op jit(solution)/shard_map/dot_general | solution.py:39
  30.0 0.0 reduce-scatter.2.cloned.1.call-update
  30.0 0.1 reshape.44
  30.1 23.5 %reduce-scatter.2.cloned.1.call-done = f32[8,6144]{1,0:T(8,128)} async-done(((f32[32,6144]{1,0:T(8,128)}), f32[8,6144]{1,0:T(8,128)}) %reduce-scatter.2.cloned.1.call-update) | async-done | bytes 196624 | tf_op jit(solution)/shard_map/reduce_scatter | solution.py:42
  53.6 0.9 multiply_convert_fusion
  54.6 15.3 %all_gather.3 = bf16[32,6144]{1,0:T(8,128)(2,1)S(1)} all-gather(bf16[8,6144]{1,0:T(8,128)(2,1)S(1)} %multiply_convert_fusion), channel_id=1, replica_groups=mesh['expert'=4,'ctx'=2,'tensor'=4] {'tensor'}, dimensions={0}, use_global_device_ids=true | all-gather | bytes 491520 | tf_op jit(solution)/shard_map/all_gather | solution.py:45
  69.8 0.1 dot_general.13
  70.0 9.6 %fusion = f32[4,2,4,1536]{3,2,1,0:T(4,128)S(1)} fusion(bf16[4,2,4,6144]{3,2,1,0:T(4,128)(2,1)S(1)} %dot_general.13, bf16[1,6144,1536]{2,1,0:T(8,128)(2,1)} %param.9), kind=kOutput, calls=%fused_computation.1 | convolution fusion | flops 603979776 | bytes 19464192 | tf_op jit(solution)/shard_map/dot_general | solution.py:44
  79.6 10.5 %all-reduce.1 = bf16[4,2,4,1536]{3,2,1,0:T(4,128)(2,1)S(1)} all-reduce(f32[4,2,4,1536]{3,2,1,0:T(4,128)S(1)} %fusion), channel_id=1, replica_groups=mesh['expert'=4,'ctx'=2,'tensor'=4] {'ctx'}, use_global_device_ids=true, to_apply=%region_4.5 | all-reduce | flops 49152 | bytes 294912 | tf_op jit(solution)/shard_map/psum | solution.py:50
  90.0 0.6 fusion.6
  90.7 3.3 %all-to-all-start.1 = ((bf16[4,4,1536]{2,1,0:T(4,128)(2,1)}), bf16[4,4,1536]{2,1,0:T(4,128)(2,1)S(1)}, u32[]{:S(2)}, u32[]{:S(2)}) async-start(bf16[4,4,1536]{2,1,0:T(4,128)(2,1)} %fusion.6), calls=%async_computation.2 | async-start | bytes 98304 | tf_op jit(solution)/shard_map/all_to_all | solution.py:52
  93.9 0.0 copy-done.1
  93.9 0.1 constant_dynamic-slice_fusion
  94.0 0.1 copy.25
  94.1 3.8 %all-to-all-done.1 = bf16[4,4,1536]{2,1,0:T(4,128)(2,1)S(1)} async-done(((bf16[4,4,1536]{2,1,0:T(4,128)(2,1)}), bf16[4,4,1536]{2,1,0:T(4,128)(2,1)S(1)}, u32[]{:S(2)}, u32[]{:S(2)}) %all-to-all-start.1) | async-done | bytes 49184 | tf_op jit(solution)/shard_map/all_to_all | solution.py:52
  98.0 0.6 gather_fusion
  98.6 0.8 multiply_reduce_fusion
  (6 shorter events, 0.1 us)
Async XLA Ops:
  6.5 2.1 %copy-start = (bf16[16,1536]{1,0:T(8,128)(2,1)S(1)}, bf16[16,1536]{1,0:T(8,128)(2,1)}, u32[]{:S(2)}) copy-start(bf16[16,1536]{1,0:T(8,128)(2,1)} %param.5) | copy-start | bytes 147460
  6.5 47.1 %reduce-scatter.2.cloned.1.call-start = ((), (), s32[]{:S(2)}) async-start(), calls=%async_computation.3 | async-start | bytes 983040 | tf_op jit(solution)/shard_map/reduce_scatter | solution.py:42
  17.2 76.8 %copy-start.1 = (f32[16,2]{0,1:T(2,128)S(1)}, f32[16,2]{0,1:T(2,128)}, u32[]{:S(2)}) copy-start(f32[16,2]{0,1:T(2,128)} %param.7) | copy-start | bytes 388
  90.7 7.3 %all-to-all-start.1 = ((bf16[4,4,1536]{2,1,0:T(4,128)(2,1)}), bf16[4,4,1536]{2,1,0:T(4,128)(2,1)S(1)}, u32[]{:S(2)}, u32[]{:S(2)}) async-start(bf16[4,4,1536]{2,1,0:T(4,128)(2,1)} %fusion.6), calls=%async_computation.2 | async-start | bytes 98304 | tf_op jit(solution)/shard_map/all_to_all | solution.py:52
Sparse Core Ops, SparseCore 0:
  30.1 23.4 reduce-scatter.1
where the time goes:
time: 107 us; the launch traced here: 106 us
  blocking collectives  34 us (32%)
  waiting for transfers between devices  27.3 us (26%)
  matrix products  22.6 us (21%)
  between operations  13.5 us (13%)
  starting transfers between devices  3.27 us (3%)
  other arithmetic  2.87 us (3%)
  local copies, waits for them, and re-layouts  2.69 us (3%)
    reduce_scatter x1, waiting for transfers between devices, local(): lax.psum_scatter(before_act, 'tensor', scatter_dimension=0, tiled=True)  23.5 us
    all_gather x1, blocking collectives, local(): lax.all_gather(hidden, 'tensor', axis=0, tiled=True)  15.3 us
    dot_general x1, matrix products, local(): lax.dot_general(row_data, up_local, (((1,), (1,)), ((), ())), preferred_e...  12.8 us
    psum x1, blocking collectives, local(): totals = lax.psum(by_block, 'ctx')  10.5 us
    dot_general x1, matrix products, local(): jnp.dot(lax.all_gather(hidden, 'tensor', axis=0, tiled=True), down_local,...  9.55 us
    all_to_all x1, blocking collectives, local(): lax.all_to_all(outgoing, 'expert', split_axis=0, concat_axis=0, tiled=True)  8.33 us
    all_to_all x1, waiting for transfers between devices, local(): lax.all_to_all(own_rows.astype(jnp.bfloat16), 'expert', split_axis=0, con...  3.83 us
    all_to_all x1, starting transfers between devices, local(): lax.all_to_all(own_rows.astype(jnp.bfloat16), 'expert', split_axis=0, con...  3.27 us
  transfers between devices with their start and end apart: 2, of which 2 were waited for; matrix products, arithmetic and copies ran while one was open for 0% of the time, Pallas kernels for 0%

commit v1 on v0

--- a/solution.py
+++ b/solution.py
@@ -2,6 +2,7 @@
 import jax.numpy as jnp
 from jax import lax
 from jax.sharding import PartitionSpec as P
+from jax.lax import all_gather
 
 
 def choice_slots(expert_ids, block_len, expert_count):
@@ -47,7 +48,7 @@
         preferred_element_type=jnp.float32,
     )
     by_block = projected.reshape(expert_count, ctx_count, capacity, width_local)
-    totals = lax.psum(by_block, "ctx")
+    totals = jnp.sum(all_gather(by_block, "ctx"), axis=0)
     own_rows = lax.dynamic_index_in_dim(totals, ctx_index, 1, keepdims=False)
     returned = lax.all_to_all(
         own_rows.astype(jnp.bfloat16), "expert", split_axis=0, concat_axis=0, tiled=True

time: 107 us -> 103 us (0.963)
  blocking collectives: 34 us -> 29.9 us
    psum x1 -> x0, blocking collectives: 10.5 us -> none  [local(): totals = lax.psum(by_block, 'ctx')]
    all_gather x0 -> x1, blocking collectives: none -> 6.34 us  [local(): totals = jnp.sum(all_gather(by_block, 'ctx'), axis=0)]
where the time goes in v1:
time: 103 us; the launch traced here: 102 us
  blocking collectives  29.9 us (29%)
  waiting for transfers between devices  27.3 us (27%)
  matrix products  22.6 us (22%)
  between operations  13.5 us (13%)
  starting transfers between devices  3.27 us (3%)
  other arithmetic  2.99 us (3%)
  local copies, waits for them, and re-layouts  2.69 us (3%)
    reduce_scatter x1, waiting for transfers between devices, local(): lax.psum_scatter(before_act, 'tensor', scatter_dimension=0, tiled=True)  23.5 us
    all_gather x1, blocking collectives, local(): lax.all_gather(hidden, 'tensor', axis=0, tiled=True)  15.3 us
    dot_general x1, matrix products, local(): lax.dot_general(row_data, up_local, (((1,), (1,)), ((), ())), preferred_e...  12.8 us
    dot_general x1, matrix products, local(): jnp.dot(lax.all_gather(hidden, 'tensor', axis=0, tiled=True), down_local,...  9.55 us
    all_to_all x1, blocking collectives, local(): lax.all_to_all(outgoing, 'expert', split_axis=0, concat_axis=0, tiled=True)  8.33 us
    all_gather x1, blocking collectives, local(): totals = jnp.sum(all_gather(by_block, 'ctx'), axis=0)  6.34 us
    all_to_all x1, waiting for transfers between devices, local(): lax.all_to_all(own_rows.astype(jnp.bfloat16), 'expert', split_axis=0, con...  3.83 us
    all_to_all x1, starting transfers between devices, local(): lax.all_to_all(own_rows.astype(jnp.bfloat16), 'expert', split_axis=0, con...  3.27 us
  transfers between devices with their start and end apart: 2, of which 2 were waited for; matrix products, arithmetic and copies ran while one was open for 0% of the time, Pallas kernels for 0%

profile of v1, /device:TPU:0, one launch (start us, length us, event | category | flops | bytes accessed | tf_op | source)
XLA Modules:
  0.0 102.3 jit_solution(10982293325440186220)
XLA Ops:
  6.5 0.0 copy-start
  6.5 0.0 reduce-scatter.2.cloned.1.call-start
  6.5 0.8 copy.32
  7.3 0.1 eq.28
  7.4 0.1 fusion.7
  7.5 0.2 select_reduce_fusion
  7.7 0.1 reshape.42
  7.8 0.1 copy.34
  7.9 0.7 add_add_fusion
  8.6 0.1 convert_reduce_fusion
  8.6 0.0 copy-done
  8.6 0.2 fusion.4
  8.8 8.3 %all_to_all.10 = bf16[4,8,1536]{2,1,0:T(8,128)(2,1)S(1)} all-to-all(bf16[4,8,1536]{2,1,0:T(8,128)(2,1)S(1)} %fusion.4), channel_id=1, replica_groups=mesh['expert'=4,'ctx'=2,'tensor'=4] {'expert'}, dimensions={0} | all-to-all | bytes 196608 | tf_op jit(solution)/shard_map/all_to_all | solution.py:36
  17.2 0.0 copy-start.1
  17.2 12.8 %fusion.2 = f32[32,6144]{1,0:T(8,128)} fusion(bf16[1,6144,1536]{2,1,0:T(8,128)(2,1)} %param.8, bf16[4,8,1536]{2,1,0:T(8,128)(2,1)S(1)} %all_to_all.10), kind=kOutput, calls=%fused_computation.3 | convolution fusion | flops 603979776 | bytes 19759104 | tf_op jit(solution)/shard_map/dot_general | solution.py:40
  30.0 0.0 reduce-scatter.2.cloned.1.call-update
  30.0 0.1 reshape.49
  30.1 23.5 %reduce-scatter.2.cloned.1.call-done = f32[8,6144]{1,0:T(8,128)} async-done(((f32[32,6144]{1,0:T(8,128)}), f32[8,6144]{1,0:T(8,128)}) %reduce-scatter.2.cloned.1.call-update) | async-done | bytes 196624 | tf_op jit(solution)/shard_map/reduce_scatter | solution.py:43
  53.6 0.9 multiply_convert_fusion
  54.6 15.3 %all_gather.6 = bf16[32,6144]{1,0:T(8,128)(2,1)S(1)} all-gather(bf16[8,6144]{1,0:T(8,128)(2,1)S(1)} %multiply_convert_fusion), channel_id=1, replica_groups=mesh['expert'=4,'ctx'=2,'tensor'=4] {'tensor'}, dimensions={0}, use_global_device_ids=true | all-gather | bytes 491520 | tf_op jit(solution)/shard_map/all_gather | solution.py:46
  69.8 0.1 reshape.45
  70.0 9.6 %fusion = f32[4,2,4,1536]{3,2,1,0:T(4,128)S(1)} fusion(bf16[4,2,4,6144]{3,2,1,0:T(4,128)(2,1)S(1)} %reshape.45, bf16[1,6144,1536]{2,1,0:T(8,128)(2,1)} %param.9), kind=kOutput, calls=%fused_computation.1 | convolution fusion | flops 603979776 | bytes 19464192 | tf_op jit(solution)/shard_map/dot_general | solution.py:45
  79.6 6.3 %all-gather = f32[8,2,4,1536]{3,2,1,0:T(4,128)S(1)} all-gather(f32[4,2,4,1536]{3,2,1,0:T(4,128)S(1)} %fusion), channel_id=2, replica_groups=mesh['expert'=4,'ctx'=2,'tensor'=4] {'ctx'}, dimensions={0}, use_global_device_ids=true | all-gather | bytes 589824 | tf_op jit(solution)/shard_map/all_gather | solution.py:51
  85.9 0.1 reduce_sum.38
  86.0 0.6 fusion.6
  86.7 3.3 %all-to-all-start.1 = ((bf16[4,4,1536]{2,1,0:T(4,128)(2,1)}), bf16[4,4,1536]{2,1,0:T(4,128)(2,1)S(1)}, u32[]{:S(2)}, u32[]{:S(2)}) async-start(bf16[4,4,1536]{2,1,0:T(4,128)(2,1)} %fusion.6), calls=%async_computation.2 | async-start | bytes 98304 | tf_op jit(solution)/shard_map/all_to_all | solution.py:53
  89.9 0.0 copy-done.1
  89.9 0.1 constant_dynamic-slice_fusion
  90.0 0.1 copy.31
  90.1 3.8 %all-to-all-done.1 = bf16[4,4,1536]{2,1,0:T(4,128)(2,1)S(1)} async-done(((bf16[4,4,1536]{2,1,0:T(4,128)(2,1)}), bf16[4,4,1536]{2,1,0:T(4,128)(2,1)S(1)}, u32[]{:S(2)}, u32[]{:S(2)}) %all-to-all-start.1) | async-done | bytes 49184 | tf_op jit(solution)/shard_map/all_to_all | solution.py:53
  94.0 0.6 gather_fusion
  94.6 0.8 multiply_reduce_fusion
  (6 shorter events, 0.1 us)
Async XLA Ops:
  6.5 2.1 %copy-start = (bf16[16,1536]{1,0:T(8,128)(2,1)S(1)}, bf16[16,1536]{1,0:T(8,128)(2,1)}, u32[]{:S(2)}) copy-start(bf16[16,1536]{1,0:T(8,128)(2,1)} %param.5) | copy-start | bytes 147460
  6.5 47.1 %reduce-scatter.2.cloned.1.call-start = ((), (), s32[]{:S(2)}) async-start(), calls=%async_computation.3 | async-start | bytes 983040 | tf_op jit(solution)/shard_map/reduce_scatter | solution.py:43
  17.2 72.8 %copy-start.1 = (f32[16,2]{0,1:T(2,128)S(1)}, f32[16,2]{0,1:T(2,128)}, u32[]{:S(2)}) copy-start(f32[16,2]{0,1:T(2,128)} %param.7) | copy-start | bytes 388
  86.7 7.3 %all-to-all-start.1 = ((bf16[4,4,1536]{2,1,0:T(4,128)(2,1)}), bf16[4,4,1536]{2,1,0:T(4,128)(2,1)S(1)}, u32[]{:S(2)}, u32[]{:S(2)}) async-start(bf16[4,4,1536]{2,1,0:T(4,128)(2,1)} %fusion.6), calls=%async_computation.2 | async-start | bytes 98304 | tf_op jit(solution)/shard_map/all_to_all | solution.py:53
Sparse Core Ops, SparseCore 0:
  30.1 23.4 reduce-scatter.1
